TPU v7x, 512 devices: a whole 4x8x8 slice. The times are simulated.
512 devices in a mesh: node: 16 (over y, core), cuts: 32 (over x, z).
Axes of the slice: x: 4, y: 8, z: 8, core: 2. Of those that a mesh axis runs over, the one named last changes fastest.
Arguments:
- transfer: float32 [16, 256, 256, 256], P('node', 'cuts'), may hold values from -0.09375 to 0.09375
- leaf_factors: float32 [16, 256, 256], P('node', 'cuts'), may hold values from -2 to 2, as said below
- node_of_slot: int32 [16], replicated, may hold values from 0 to 15, each once
Outputs:
- basis: float32 [16, 256, 256, 256], P('node', None, 'cuts')
- r_factor: float32 [16, 256, 256], P('node', 'cuts')
Inputs may be any that keep to these rules, and one draw needn't show every extreme that they name: `leaf_factors`: each slice is upper triangular with its diagonal from 0.5 to 2.
All inputs are finite; a program needn't handle non-finite values.
Results may differ from a plain program's by a relative error of at most 0.0003.
Values sent between devices are 32-bit elements; how exact they have to be, the bound alone decides.
No kernel may reach another device: no remote copies, remote signals or barrier semaphores. Data moves between devices by JAX's collectives and lax.ppermute only.
A program may use at most 64 MiB of HBM per device.

v0:
```python
import jax
import jax.numpy as jnp
from jax import lax
from jax.sharding import PartitionSpec as P

HIGHEST = lax.Precision.HIGHEST


def laid_out(pieces, dim):
    lengths = list(pieces.shape[1:])
    lengths[dim] *= pieces.shape[0]
    return jnp.moveaxis(pieces, 0, dim).reshape(lengths)


def from_everyone(array, axis):
    count = lax.axis_size(axis)
    return lax.all_to_all(
        jnp.broadcast_to(array[None], (count, *array.shape)), axis, 0, 0, tiled=True
    )


def collect(array, axis, dim):
    return laid_out(from_everyone(array, axis), dim)


def filled_up(lines, count):
    spare = -len(lines) % count
    return jnp.pad(lines, [(0, spare)] + [(0, 0)] * (lines.ndim - 1))


def cut_along(array, dim, count):
    before, after = (array.shape[:dim], array.shape[dim + 1 :])
    return jnp.moveaxis(array.reshape(*before, count, -1, *after), dim, 0)


def sent_and_summed(array, axis, dim):
    count = lax.axis_size(axis)
    pieces = lax.all_to_all(cut_along(array, dim, count), axis, 0, 0, tiled=True)
    return jnp.sum(pieces, axis=0)


def sum_by_parts(array, axes):
    lines = array.reshape(-1, array.shape[-1])
    padded = filled_up(lines, lax.axis_size(axes))
    whole = collect(sent_and_summed(padded, axes, 0), axes, 0)
    return lax.slice_in_dim(whole, 0, len(lines)).reshape(array.shape)


def pick_rows(factor_table, wanted):
    piece_count = factor_table.shape[0]
    onehot = (wanted[:, None] == lax.iota(jnp.int32, piece_count)[None, :]).astype(jnp.float32)
    return jnp.einsum("cs,srk->crk", onehot, factor_table, precision=HIGHEST)


def route_children(rows_here, wanted):
    factor_table = collect(rows_here[None], "node", 0)
    picked = pick_rows(factor_table, wanted)
    return collect(picked, "cuts", 1)


def contract_regroup(tensor, left_factor, right_factor):
    halfway = jnp.einsum("xa,pab->pxb", left_factor, tensor, precision=HIGHEST)
    mixed_tensor = jnp.einsum("yb,pxb->pxy", right_factor, halfway, precision=HIGHEST)
    return lax.all_to_all(mixed_tensor, "cuts", split_axis=1, concat_axis=0, tiled=True)


def shards(transfer, leaf_factors, node_of_slot):
    slot_count = lax.axis_size("node")
    cut_count = lax.axis_size("cuts")
    group_index = lax.axis_index("node")
    member_index = lax.axis_index("cuts")
    tensor = transfer[0]
    rank_size = tensor.shape[1]
    row_count = rank_size // cut_count
    slot_ids = lax.iota(jnp.int32, slot_count)
    node_id = node_of_slot[group_index]
    slot_of = jnp.sum(
        jnp.where(node_of_slot[None, :] == slot_ids[:, None], slot_ids[None, :], 0), axis=1
    )
    log_slots = slot_count.bit_length() - 1
    my_depth = jnp.zeros((), jnp.int32)
    for level_bit in range(1, log_slots):
        my_depth = my_depth + (node_id >= 2**level_bit).astype(jnp.int32)
    children = jnp.stack([2 * node_id, 2 * node_id + 1]) % slot_count
    rows_here = leaf_factors[0]
    saved_flat = jnp.zeros((rank_size, row_count * rank_size), jnp.float32)
    saved_lower = jnp.eye(rank_size, dtype=jnp.float32)
    saved_upper = jnp.zeros((rank_size, rank_size), jnp.float32)
    for level_now in range(log_slots - 1, 0, -1):
        if level_now == log_slots - 1:
            wanted = children
        else:
            wanted = slot_of[children]
        factors = route_children(rows_here, wanted)
        mixed_rows = contract_regroup(tensor, factors[0], factors[1])
        flat_rows = mixed_rows.reshape(rank_size, row_count * rank_size)
        partial_gram = jnp.dot(
            flat_rows, flat_rows.T, precision=HIGHEST, preferred_element_type=jnp.float32
        )
        gram_matrix = sum_by_parts(partial_gram, "cuts")
        lower_factor = jnp.linalg.cholesky(gram_matrix)
        upper_factor = lower_factor.T
        active = my_depth == level_now
        saved_flat = jnp.where(active, flat_rows, saved_flat)
        saved_lower = jnp.where(active, lower_factor, saved_lower)
        saved_upper = jnp.where(active, upper_factor, saved_upper)
        rows_here = lax.dynamic_slice_in_dim(upper_factor, member_index * row_count, row_count, 0)
    solved = jax.scipy.linalg.solve_triangular(saved_lower, saved_flat, lower=True)
    basis_rows = (rank_size * solved).reshape(1, rank_size, row_count, rank_size)
    upper_rows = lax.dynamic_slice_in_dim(saved_upper, member_index * row_count, row_count, 0)[None]
    return (basis_rows, upper_rows)


def solution(mesh):
    placed = (P("node", "cuts", None, None), P("node", "cuts", None), P())
    return jax.shard_map(
        shards,
        mesh=mesh,
        in_specs=placed,
        out_specs=(P("node", None, "cuts", None), P("node", "cuts", None)),
        check_vma=False,
    )
```

profile of v0, /device:TPU:64, one launch (start us, length us, event | category | flops | bytes accessed | tf_op | source)
XLA Modules:
  0.0 560.9 jit_solution(2473077335006058042)
XLA Ops:
  0.6 1.5 broadcast_in_dim.40
  2.2 7.2 %all-to-all-start = ((f32[16,1,8,256]{3,2,1,0:T(8,128)}), f32[16,1,8,256]{3,2,1,0:T(8,128)S(1)}, u32[]{:S(2)}, u32[]{:S(2)}) async-start(f32[16,1,8,256]{3,2,1,0:T(8,128)} %broadcast_in_dim.40), calls=%async_computation | async-start | bytes 262144 | tf_op jit(solution)/shard_map/all_to_all | solution.py:17
  9.4 1.2 dynamic_slice.12
  11.4 6.7 %all-to-all-done = f32[16,1,8,256]{3,2,1,0:T(8,128)S(1)} async-done(((f32[16,1,8,256]{3,2,1,0:T(8,128)}), f32[16,1,8,256]{3,2,1,0:T(8,128)S(1)}, u32[]{:S(2)}, u32[]{:S(2)}) %all-to-all-start) | async-done | bytes 131104 | tf_op jit(solution)/shard_map/all_to_all | solution.py:17
  18.3 30.9 %all_to_all.105 = f32[32,2,8,256]{3,2,1,0:T(8,128)S(1)} all-to-all(f32[32,2,8,256]{3,2,1,0:T(8,128)S(1)} %broadcast_in_dim.41), channel_id=1, replica_groups=mesh['node'=16,'cuts'=32] {'cuts'}, dimensions={0} | all-to-all | bytes 1048576 | tf_op jit(solution)/shard_map/all_to_all | solution.py:17
  49.2 1.9 fusion.13
  51.1 3.0 fusion.11
  54.1 55.3 %all_to_all.106 = f32[8,256,256]{2,0,1:T(8,128)S(1)} all-to-all(f32[8,256,256]{2,0,1:T(8,128)S(1)} %fusion.11), channel_id=1, replica_groups=mesh['node'=16,'cuts'=32] {'cuts'}, dimensions={1} | all-to-all | bytes 4194304 | tf_op jit(solution)/shard_map/all_to_all | solution.py:64
  109.4 1.9 fusion.67
  111.3 16.8 %all_to_all.107 = f32[32,8,256]{2,1,0:T(8,128)S(1)} all-to-all(f32[32,8,256]{2,1,0:T(8,128)S(1)} %fusion.67), channel_id=1, replica_groups=mesh['node'=16,'cuts'=32] {'cuts'}, dimensions={0} | all-to-all | bytes 524288 | tf_op jit(solution)/shard_map/all_to_all | solution.py:38
  128.1 0.7 broadcast_in_dim.42
  128.8 4.8 all-to-all-start.4
  133.7 11.1 %all-to-all-done.4 = f32[32,8,256]{2,1,0:T(8,128)S(1)} async-done(((f32[32,8,256]{2,1,0:T(8,128)}), f32[32,8,256]{2,1,0:T(8,128)S(1)}, u32[]{:S(2)}, u32[]{:S(2)}) %all-to-all-start.4) | async-done | bytes 262176 | tf_op jit(solution)/shard_map/all_to_all | solution.py:17
  145.0 11.7 %cholesky.172 = f32[128,128]{1,0:T(8,128)S(1)} custom-call(f32[128,128]{1,0:T(8,128)S(1)} %cholesky.270), custom_call_target="Cholesky" | custom-call | tf_op jit(solution)/shard_map/jit(cholesky)/cholesky | solution.py:101
  156.8 9.8 %custom-call.15 = f32[1,128,128]{1,2,0:T(8,128)S(1)} custom-call(f32[1,128,128]{2,1,0:T(8,128)S(1)} %get-tuple-element.42), custom_call_target="InvertDiagBlocksLowerTriangular" | custom-call | tf_op jit(solution)/shard_map/jit(cholesky)/cholesky | solution.py:101
  167.3 11.7 %cholesky.189 = f32[128,128]{1,0:T(8,128)S(1)} custom-call(f32[128,128]{1,0:T(8,128)S(1)} %convolution_subtract_fusion.3), custom_call_target="Cholesky" | custom-call | tf_op jit(solution)/shard_map/jit(cholesky)/cholesky | solution.py:101
  179.1 0.7 compare_reduce_fusion.4
  181.1 0.7 copy-done.5
  181.9 0.7 broadcast_in_dim.43
  182.6 3.5 all-to-all-start.5
  186.3 0.6 gather_fusion
  187.0 7.8 %all-to-all-done.5 = f32[16,1,8,256]{3,2,1,0:T(8,128)S(1)} async-done(((f32[16,1,8,256]{3,2,1,0:T(8,128)}), f32[16,1,8,256]{3,2,1,0:T(8,128)S(1)}, u32[]{:S(2)}, u32[]{:S(2)}) %all-to-all-start.5) | async-done | bytes 131104 | tf_op jit(solution)/shard_map/all_to_all | solution.py:17
  195.0 23.0 %all_to_all.108 = f32[32,2,8,256]{3,2,1,0:T(8,128)S(1)} all-to-all(f32[32,2,8,256]{3,2,1,0:T(8,128)S(1)} %broadcast_in_dim.44), channel_id=1, replica_groups=mesh['node'=16,'cuts'=32] {'cuts'}, dimensions={0} | all-to-all | bytes 1048576 | tf_op jit(solution)/shard_map/all_to_all | solution.py:17
  218.1 1.9 fusion.16
  220.0 3.0 fusion.9
  223.0 55.6 %all_to_all.109 = f32[8,256,256]{2,0,1:T(8,128)S(1)} all-to-all(f32[8,256,256]{2,0,1:T(8,128)S(1)} %fusion.9), channel_id=1, replica_groups=mesh['node'=16,'cuts'=32] {'cuts'}, dimensions={1} | all-to-all | bytes 4194304 | tf_op jit(solution)/shard_map/all_to_all | solution.py:64
  278.5 1.9 fusion.68
  280.4 16.8 %all_to_all.110 = f32[32,8,256]{2,1,0:T(8,128)S(1)} all-to-all(f32[32,8,256]{2,1,0:T(8,128)S(1)} %fusion.68), channel_id=1, replica_groups=mesh['node'=16,'cuts'=32] {'cuts'}, dimensions={0} | all-to-all | bytes 524288 | tf_op jit(solution)/shard_map/all_to_all | solution.py:38
  297.3 16.0 %all_to_all.111 = f32[32,8,256]{2,1,0:T(8,128)S(1)} all-to-all(f32[32,8,256]{2,1,0:T(8,128)S(1)} %broadcast_in_dim.45), channel_id=1, replica_groups=mesh['node'=16,'cuts'=32] {'cuts'}, dimensions={0} | all-to-all | bytes 524288 | tf_op jit(solution)/shard_map/all_to_all | solution.py:17
  313.5 11.7 %cholesky.206 = f32[128,128]{1,0:T(8,128)S(1)} custom-call(f32[128,128]{1,0:T(8,128)S(1)} %cholesky.273), custom_call_target="Cholesky" | custom-call | tf_op jit(solution)/shard_map/jit(cholesky)/cholesky | solution.py:101
  325.3 9.8 %custom-call.16 = f32[1,128,128]{1,2,0:T(8,128)S(1)} custom-call(f32[1,128,128]{2,1,0:T(8,128)S(1)} %get-tuple-element.38), custom_call_target="InvertDiagBlocksLowerTriangular" | custom-call | tf_op jit(solution)/shard_map/jit(cholesky)/cholesky | solution.py:101
  335.8 11.7 %cholesky.223 = f32[128,128]{1,0:T(8,128)S(1)} custom-call(f32[128,128]{1,0:T(8,128)S(1)} %convolution_subtract_fusion.2), custom_call_target="Cholesky" | custom-call | tf_op jit(solution)/shard_map/jit(cholesky)/cholesky | solution.py:101
  347.5 0.6 compare_reduce_fusion.2
  350.1 0.7 copy-done.6
  351.0 11.2 %all_to_all.112 = f32[16,1,8,256]{3,2,1,0:T(8,128)S(1)} all-to-all(f32[16,1,8,256]{3,2,1,0:T(8,128)S(1)} %broadcast_in_dim.46), channel_id=1, replica_groups=mesh['node'=16,'cuts'=32] {'node'}, dimensions={0} | all-to-all | bytes 262144 | tf_op jit(solution)/shard_map/all_to_all | solution.py:17
  362.5 23.0 %all_to_all.113 = f32[32,2,8,256]{3,2,1,0:T(8,128)S(1)} all-to-all(f32[32,2,8,256]{3,2,1,0:T(8,128)S(1)} %broadcast_in_dim.47), channel_id=1, replica_groups=mesh['node'=16,'cuts'=32] {'cuts'}, dimensions={0} | all-to-all | bytes 1048576 | tf_op jit(solution)/shard_map/all_to_all | solution.py:17
  385.5 1.9 fusion.19
  387.4 3.0 fusion.7
  390.4 55.6 %all_to_all.114 = f32[8,256,256]{2,0,1:T(8,128)S(1)} all-to-all(f32[8,256,256]{2,0,1:T(8,128)S(1)} %fusion.7), channel_id=1, replica_groups=mesh['node'=16,'cuts'=32] {'cuts'}, dimensions={1} | all-to-all | bytes 4194304 | tf_op jit(solution)/shard_map/all_to_all | solution.py:64
  445.9 1.3 copy-done.3
  447.3 2.6 fusion.69
  449.8 5.2 all-to-all-start.13
  457.0 9.8 %all-to-all-done.13 = f32[32,8,256]{2,1,0:T(8,128)S(1)} async-done(((f32[32,8,256]{2,1,0:T(8,128)}), f32[32,8,256]{2,1,0:T(8,128)S(1)}, u32[]{:S(2)}, u32[]{:S(2)}) %all-to-all-start.13) | async-done | bytes 262176 | tf_op jit(solution)/shard_map/all_to_all | solution.py:38
  466.9 0.7 broadcast_in_dim.48
  467.6 4.9 all-to-all-start.14
  472.5 3.6 select_select_fusion
  476.1 7.5 %all-to-all-done.14 = f32[32,8,256]{2,1,0:T(8,128)S(1)} async-done(((f32[32,8,256]{2,1,0:T(8,128)}), f32[32,8,256]{2,1,0:T(8,128)S(1)}, u32[]{:S(2)}, u32[]{:S(2)}) %all-to-all-start.14) | async-done | bytes 262176 | tf_op jit(solution)/shard_map/all_to_all | solution.py:17
  483.8 11.7 %cholesky.240 = f32[128,128]{1,0:T(8,128)S(1)} custom-call(f32[128,128]{1,0:T(8,128)S(1)} %cholesky.276), custom_call_target="Cholesky" | custom-call | tf_op jit(solution)/shard_map/jit(cholesky)/cholesky | solution.py:101
  495.6 9.8 %custom-call.17 = f32[1,128,128]{1,2,0:T(8,128)S(1)} custom-call(f32[1,128,128]{2,1,0:T(8,128)S(1)} %get-tuple-element.34), custom_call_target="InvertDiagBlocksLowerTriangular" | custom-call | tf_op jit(solution)/shard_map/jit(cholesky)/cholesky | solution.py:101
  506.1 11.7 %cholesky.257 = f32[128,128]{1,0:T(8,128)S(1)} custom-call(f32[128,128]{1,0:T(8,128)S(1)} %convolution_subtract_fusion.1), custom_call_target="Cholesky" | custom-call | tf_op jit(solution)/shard_map/jit(cholesky)/cholesky | solution.py:101
  517.9 0.7 compare_reduce_fusion
  520.5 1.1 fusion.27
  521.6 0.7 copy.88
  522.4 4.1 while.1
  522.4 0.7 fusion.85
  523.0 1.3 bitcast_dynamic-update-slice_fusion.2
  524.4 0.7 fusion.85
  525.1 1.3 bitcast_dynamic-update-slice_fusion.2
  527.1 20.7 %custom-call.12 = f32[2,128,128]{1,2,0:T(8,128)S(1)} custom-call(f32[2,128,128]{2,1,0:T(8,128)} %copy-done.7), custom_call_target="InvertDiagBlocksLowerTriangular" | custom-call | tf_op jit(solution)/shard_map/jit(_solve_triangular)/triangular_solve | solution.py:108
  547.8 2.4 fusion.22
  550.2 2.0 fusion
  552.2 2.5 copy.97
  554.7 2.3 convolution_bitcast_fusion
  557.9 2.5 copy.87
  (80 shorter events, 7.4 us)
Async XLA Ops:
  0.6 48.6 %copy-start = (f32[1,8,256,256]{3,2,1,0:T(8,128)S(1)}, f32[1,8,256,256]{3,2,1,0:T(8,128)}, u32[]{:S(2)}) copy-start(f32[1,8,256,256]{3,2,1,0:T(8,128)} %param.4) | copy-start | bytes 6291460
  2.2 15.9 %all-to-all-start = ((f32[16,1,8,256]{3,2,1,0:T(8,128)}), f32[16,1,8,256]{3,2,1,0:T(8,128)S(1)}, u32[]{:S(2)}, u32[]{:S(2)}) async-start(f32[16,1,8,256]{3,2,1,0:T(8,128)} %broadcast_in_dim.40), calls=%async_computation | async-start | bytes 262144 | tf_op jit(solution)/shard_map/all_to_all | solution.py:17
  109.4 1.9 copy-start.1
  128.8 16.0 %all-to-all-start.4 = ((f32[32,8,256]{2,1,0:T(8,128)}), f32[32,8,256]{2,1,0:T(8,128)S(1)}, u32[]{:S(2)}, u32[]{:S(2)}) async-start(f32[32,8,256]{2,1,0:T(8,128)} %broadcast_in_dim.42), calls=%async_computation.4 | async-start | bytes 524288 | tf_op jit(solution)/shard_map/all_to_all | solution.py:17
  133.7 52.5 %copy-start.8 = (s32[16]{0:T(128)S(1)}, s32[16]{0:T(128)}, u32[]{:S(2)}) copy-start(s32[16]{0:T(128)} %param.6) | copy-start | bytes 196
  181.1 0.7 copy-start.5
  182.6 12.1 %all-to-all-start.5 = ((f32[16,1,8,256]{3,2,1,0:T(8,128)}), f32[16,1,8,256]{3,2,1,0:T(8,128)S(1)}, u32[]{:S(2)}, u32[]{:S(2)}) async-start(f32[16,1,8,256]{3,2,1,0:T(8,128)} %broadcast_in_dim.43), calls=%async_computation.5 | async-start | bytes 262144 | tf_op jit(solution)/shard_map/all_to_all | solution.py:17
  278.5 1.9 copy-start.2
  350.1 0.7 copy-start.6
  445.9 1.3 copy-start.3
  449.8 17.0 %all-to-all-start.13 = ((f32[32,8,256]{2,1,0:T(8,128)}), f32[32,8,256]{2,1,0:T(8,128)S(1)}, u32[]{:S(2)}, u32[]{:S(2)}) async-start(f32[32,8,256]{2,1,0:T(8,128)} %fusion.69), calls=%async_computation.13 | async-start | bytes 524288 | tf_op jit(solution)/shard_map/all_to_all | solution.py:38
  467.6 16.0 %all-to-all-start.14 = ((f32[32,8,256]{2,1,0:T(8,128)}), f32[32,8,256]{2,1,0:T(8,128)S(1)}, u32[]{:S(2)}, u32[]{:S(2)}) async-start(f32[32,8,256]{2,1,0:T(8,128)} %broadcast_in_dim.48), calls=%async_computation.14 | async-start | bytes 524288 | tf_op jit(solution)/shard_map/all_to_all | solution.py:17
  526.4 0.6 copy-start.7
  547.8 2.4 copy-start.4
where the time goes:
time: 569 us; the launch traced here: 561 us
  blocking collectives  304 us (53%)
  other arithmetic  130 us (23%)
  waiting for transfers between devices  42.9 us (8%)
  matrix products  30 us (5%)
  starting transfers between devices  25.6 us (4%)
  local copies, waits for them, and re-layouts  20.6 us (4%)
  between operations  8.01 us (1%)
    all_to_all x3, blocking collectives, contract_regroup(): lax.all_to_all(mixed_tensor, 'cuts', split_axis=1, concat_axis=0, tiled=T...  166 us
    all_to_all x5, blocking collectives, from_everyone(): lax.all_to_all(jnp.broadcast_to(array[None], (count, *array.shape)), axis...  104 us
    another operation x20, other arithmetic, shards(): lower_factor = jnp.linalg.cholesky(gram_matrix)  103 us
    all_to_all x2, blocking collectives, sent_and_summed(): lax.all_to_all(cut_along(array, dim, count), axis, 0, 0, tiled=True)  33.6 us
    all_to_all x4, waiting for transfers between devices, from_everyone(): lax.all_to_all(jnp.broadcast_to(array[None], (count, *array.shape)), axis...  33.1 us
    another operation x3, other arithmetic, shards(): jax.scipy.linalg.solve_triangular(saved_lower, saved_flat, lower=True)  20.8 us
    all_to_all x4, starting transfers between devices, from_everyone(): lax.all_to_all(jnp.broadcast_to(array[None], (count, *array.shape)), axis...  20.4 us
  transfers between devices with their start and end apart: 5, of which 5 were waited for; matrix products, arithmetic and copies ran while one was open for 1% of the time, Pallas kernels for 0%

commit v1 on v0

v1 whole, which is shorter than its diff:
```python
import functools

import jax
import jax.numpy as jnp
from jax import lax
from jax.experimental import pallas as pl
from jax.experimental.pallas import tpu as pltpu
from jax.sharding import PartitionSpec as P

HIGHEST = lax.Precision.HIGHEST
TILE = 8
LANES = 128
PANEL = 64
GROUP = 16
VMEM = pltpu.VMEM
PARAMS = pltpu.CompilerParams(vmem_limit_bytes=16 * 2**20)


def from_everyone(array, axis):
    count = lax.axis_size(axis)
    return lax.all_to_all(
        jnp.broadcast_to(array[None], (count, *array.shape)), axis, 0, 0, tiled=True
    )


def product(left, right, contracted):
    return lax.dot_general(
        left,
        right,
        ((contracted[:1], contracted[1:]), ((), ())),
        precision=HIGHEST,
        preferred_element_type=jnp.float32,
    )


def eliminate(tiles, first):
    count, width = len(tiles), tiles[0].shape[1]
    lines = lax.broadcasted_iota(jnp.int32, (TILE, LANES), 0)
    tiles = list(tiles)
    for start in range(0, count * TILE, GROUP):
        top = start // TILE
        copies = [
            [
                jnp.broadcast_to(tile[:, first + start + i : first + start + i + 1], (TILE, LANES))
                for tile in tiles[top:]
            ]
            for i in range(GROUP)
        ]
        for i in range(GROUP):
            home, line = divmod(start + i, TILE)
            low = home if line < TILE - 1 else home + 1
            inverse = 1.0 / copies[i][home - top][line : line + 1, :]
            factors = {}
            for t in range(low, count):
                factor = copies[i][t - top] * inverse
                factors[t] = jnp.where(lines > line, factor, 0.0) if t == home else factor
            for later in range(i + 1, GROUP):
                row = copies[later][home - top][line : line + 1, :]
                for t in range(low, count):
                    copies[later][t - top] = copies[later][t - top] - factors[t] * row
            row = tiles[home][line : line + 1, :]
            for t in range(low, count):
                wide = jnp.concatenate([factors[t]] * (width // LANES), axis=1)
                tiles[t] = tiles[t] - wide * row
    return tiles


def factor_gram(read_rows, size, work_ref, with_inverse=False):
    for first in range(0, size, PANEL):
        rows = pl.ds(first, PANEL)
        begin, end = first // LANES * LANES, size
        block = read_rows(first)[:, begin:]
        row_ids = lax.broadcasted_iota(jnp.int32, (PANEL, size), 0) + first
        column_ids = lax.broadcasted_iota(jnp.int32, (PANEL, size), 1)
        if with_inverse:
            reach = -(-(first + PANEL) // LANES) * LANES
            end = size + reach
            unit = (row_ids == column_ids).astype(jnp.float32)
            block = jnp.concatenate([block, unit[:, :reach]], axis=1)
        if first:
            block = block - product(
                work_ref[0:first, first : first + PANEL], work_ref[0:first, begin:end], (0, 0)
            )
        tiles = [block[t : t + TILE, :] for t in range(0, PANEL, TILE)]
        block = jnp.concatenate(eliminate(tiles, first - begin), axis=0)
        square = block[:, : size - begin]
        ahead = column_ids[:, begin:] - row_ids[:, begin:]
        pivots = jnp.sum(jnp.where(ahead == 0, square, 0.0), axis=1, keepdims=True)
        scale = lax.rsqrt(pivots)
        work_ref[rows, begin:size] = jnp.where(ahead >= 0, square * scale, 0.0)
        if begin:
            work_ref[rows, 0:begin] = jnp.zeros((PANEL, begin), jnp.float32)
        if with_inverse:
            work_ref[rows, size:end] = block[:, size - begin :] * scale
            if end < 2 * size:
                work_ref[rows, end:] = jnp.zeros((PANEL, 2 * size - end), jnp.float32)


def child_rows(gathered_ref, side):
    size = gathered_ref.shape[-1]

    def read_rows(first):
        members = pl.ds(first // TILE, PANEL // TILE)
        return gathered_ref[members, side].reshape(PANEL, size)

    return read_rows


def mix_tensor(left, tensor_ref, out_ref):
    count, size, _ = tensor_ref.shape
    for p in range(count):
        mixed = product(left, tensor_ref[p], (1, 0))
        for block in range(size // TILE):
            for half in range(size // LANES):
                out_ref[block, pl.ds(half * TILE * count + p, TILE, stride=count), :] = mixed[
                    block * TILE : (block + 1) * TILE, half * LANES : (half + 1) * LANES
                ]


def leaf_left_kernel(gathered_ref, tensor_ref, out_ref):
    size = tensor_ref.shape[1]
    mix_tensor(gathered_ref[:, 0].reshape(size, size), tensor_ref, out_ref)


def inner_left_kernel(gathered_ref, tensor_hbm, out_ref, tensor_ref, work_ref, done):
    size = tensor_ref.shape[1]
    copy = pltpu.make_async_copy(tensor_hbm, tensor_ref, done)
    copy.start()
    factor_gram(child_rows(gathered_ref, 0), size, work_ref)
    copy.wait()
    mix_tensor(work_ref[...], tensor_ref, out_ref)


def mix_left(gathered, tensor, inner):
    count, size, _ = tensor.shape
    result = jax.ShapeDtypeStruct((size // TILE, size * count // 16, LANES), jnp.float32)
    whole = pl.BlockSpec(memory_space=VMEM)
    mixed = pl.pallas_call(
        inner_left_kernel if inner else leaf_left_kernel,
        in_specs=[whole, pl.BlockSpec(memory_space=pl.ANY) if inner else whole],
        out_shape=result,
        scratch_shapes=[
            VMEM(tensor.shape, jnp.float32),
            VMEM((size, size), jnp.float32),
            pltpu.SemaphoreType.DMA(()),
        ]
        if inner
        else [],
        compiler_params=PARAMS,
        name="mix_left",
    )(gathered, tensor)
    return lax.all_to_all(mixed, "cuts", 0, 0, tiled=True)


def right_factor_kernel(gathered_ref, out_ref):
    size = out_ref.shape[0]
    factor_gram(child_rows(gathered_ref, 1), size, out_ref)


def right_factor(gathered):
    size = gathered.shape[-1]
    return pl.pallas_call(
        right_factor_kernel,
        out_shape=jax.ShapeDtypeStruct((size, size), jnp.float32),
        cost_estimate=pl.CostEstimate(
            flops=8 * 10**9, bytes_accessed=3 * 4 * size * size, transcendentals=size
        ),
        compiler_params=PARAMS,
        name="right_factor",
    )(gathered)


def mix_right_kernel(right_ref, halfway_ref, mixed_ref, gram_ref):
    size = gram_ref.shape[0]
    if len(right_ref.shape) == 4:
        right = right_ref[:, 1].reshape(size, size)
    else:
        right = right_ref[...]
    lines = mixed_ref.shape[0]
    parents = halfway_ref.shape[1] // (lines * (size // LANES))
    for x in range(lines):
        halves = []
        for half in range(size // LANES):
            rows = pl.ds((half * lines + x) * parents, parents)
            halves.append(halfway_ref[:, rows, :].reshape(size, LANES))
        mixed = product(jnp.concatenate(halves, axis=1), right, (1, 1))
        mixed_ref[x] = mixed
        term = product(mixed, mixed, (1, 1))
        gram_ref[...] = term if x == 0 else gram_ref[...] + term


def mix_right(halfway, right):
    size = right.shape[-1]
    mixed, partial = pl.pallas_call(
        mix_right_kernel,
        out_shape=[
            jax.ShapeDtypeStruct((TILE, size, size), jnp.float32),
            jax.ShapeDtypeStruct((size, size), jnp.float32),
        ],
        compiler_params=PARAMS,
        name="mix_right",
    )(right, halfway)
    cut_count = lax.axis_size("cuts")
    pieces = lax.all_to_all(
        partial.reshape(cut_count, size // cut_count, size), "cuts", 0, 0, tiled=True
    )
    return mixed, jnp.sum(pieces, axis=0)


def last_kernel(place_ref, gathered_ref, mixed_hbm, basis_ref, upper_ref, mixed_ref, work_ref, wide_ref, done):
    size = mixed_ref.shape[1]
    lines = mixed_ref.shape[0]
    copy = pltpu.make_async_copy(mixed_hbm, mixed_ref, done)
    copy.start()

    def read_rows(first):
        members = pl.ds(first // TILE, PANEL // TILE)
        return gathered_ref[members].reshape(PANEL, size)

    factor_gram(read_rows, size, work_ref, with_inverse=True)
    active = place_ref[1] > 0
    mine = pl.ds(pl.multiple_of(place_ref[0] * TILE, TILE), TILE)
    upper_ref[...] = jnp.where(active, work_ref[mine, 0:size], 0.0)
    inverse = jnp.where(active, work_ref[:, size:] * size, 0.0)
    copy.wait()
    for x in range(lines):
        solved = product(inverse, mixed_ref[x], (1, 0))
        for half in range(size // LANES):
            wide_ref[half, pl.ds(x, size, stride=lines), :] = solved[:, half * LANES : (half + 1) * LANES]
    for half in range(size // LANES):
        basis_ref[:, :, half * LANES : (half + 1) * LANES] = wide_ref[half].reshape(size, lines, LANES)


def last(place, gathered, mixed):
    lines, size, _ = mixed.shape
    whole = pl.BlockSpec(memory_space=VMEM)
    return pl.pallas_call(
        last_kernel,
        in_specs=[
            pl.BlockSpec(memory_space=pltpu.SMEM),
            whole,
            pl.BlockSpec(memory_space=pl.ANY),
        ],
        out_specs=[whole, whole],
        out_shape=[
            jax.ShapeDtypeStruct((size, lines, size), jnp.float32),
            jax.ShapeDtypeStruct((TILE, size), jnp.float32),
        ],
        scratch_shapes=[
            VMEM(mixed.shape, jnp.float32),
            VMEM((size, 2 * size), jnp.float32),
            VMEM((size // LANES, size * lines, LANES), jnp.float32),
            pltpu.SemaphoreType.DMA(()),
        ],
        compiler_params=PARAMS,
        name="last",
    )(place, gathered, mixed)


def pick_children(rows_here, chosen):
    table = from_everyone(rows_here, "node")
    picked = [jnp.sum(jnp.where(mask[:, None, None], table, 0.0), axis=0) for mask in chosen]
    return jnp.stack(picked)


def shards(transfer, leaf_factors, node_of_slot):
    slot_count = lax.axis_size("node")
    group_index = lax.axis_index("node")
    member_index = lax.axis_index("cuts")
    tensor = transfer[0]
    slot_ids = lax.iota(jnp.int32, slot_count)
    node_id = jnp.sum(jnp.where(slot_ids == group_index, node_of_slot, 0))
    log_slots = slot_count.bit_length() - 1
    my_depth = jnp.zeros((), jnp.int32)
    for level_bit in range(1, log_slots):
        my_depth = my_depth + (node_id >= 2**level_bit).astype(jnp.int32)
    children = [(2 * node_id + side) % slot_count for side in range(2)]
    place = jnp.stack([member_index.astype(jnp.int32), my_depth])

    rows = pick_children(leaf_factors[0], [slot_ids == child for child in children])
    gathered = from_everyone(rows, "cuts")
    halfway = mix_left(gathered, tensor, inner=False)
    mixed, rows_here = mix_right(halfway, gathered)

    def process(rows, tensor, mixed, rows_here):
        gathered = from_everyone(rows, "cuts")
        halfway = mix_left(gathered, tensor, inner=True)
        return mix_right(halfway, right_factor(gathered))

    def keep(rows, tensor, mixed, rows_here):
        return mixed, rows_here

    for level_now in range(log_slots - 2, 0, -1):
        rows = pick_children(rows_here, [node_of_slot == child for child in children])
        mixed, rows_here = lax.cond(
            my_depth == level_now, process, keep, rows, tensor, mixed, rows_here
        )

    gathered = from_everyone(rows_here, "cuts")
    basis, upper = last(place, gathered, mixed)
    return basis[None], upper[None]


def solution(mesh):
    placed = (P("node", "cuts", None, None), P("node", "cuts", None), P())
    return jax.shard_map(
        shards,
        mesh=mesh,
        in_specs=placed,
        out_specs=(P("node", None, "cuts", None), P("node", "cuts", None)),
        check_vma=False,
    )
```

time: 569 us -> 371 us (0.65)
  the two profiles are of different devices: /device:TPU:64 before, /device:TPU:56 now
where the time goes in v1:
time: 371 us; the launch traced here: 378 us
  starting transfers between devices  138 us (37%)
  blocking collectives  136 us (37%)
  waiting for transfers between devices  45.6 us (12%)
  Pallas kernels  41 us (11%)
  loops' own time  6.73 us (2%)
  local copies, waits for them, and re-layouts  4.98 us (1%)
  between operations  3.92 us (1%)
    all_to_all x4, starting transfers between devices, from_everyone(): lax.all_to_all(jnp.broadcast_to(array[None], (count, *array.shape)), axis...  132 us
    all_to_all x1, blocking collectives, mix_left(): return lax.all_to_all(mixed, 'cuts', 0, 0, tiled=True)  56.5 us
    all_to_all x2, blocking collectives, from_everyone(): lax.all_to_all(jnp.broadcast_to(array[None], (count, *array.shape)), axis...  45.9 us
    all_to_all x2, blocking collectives, mix_right(): lax.all_to_all(partial.reshape(cut_count, size // cut_count, size), 'cuts...  33.5 us
    all_to_all x4, waiting for transfers between devices, from_everyone(): lax.all_to_all(jnp.broadcast_to(array[None], (count, *array.shape)), axis...  23.8 us
    all_to_all x1, waiting for transfers between devices, mix_left(): return lax.all_to_all(mixed, 'cuts', 0, 0, tiled=True)  21.9 us
    pallas_call x1, Pallas kernels, last(): pl.pallas_call(last_kernel, in_specs=[pl.BlockSpec(memory_space=pltpu.SME...  12.4 us
    pallas_call x2, Pallas kernels, mix_left(): pl.pallas_call(inner_left_kernel if inner else leaf_left_kernel, in_specs...  12.1 us
  transfers between devices with their start and end apart: 5, of which 5 were waited for; matrix products, arithmetic and copies ran while one was open for 0% of the time, Pallas kernels for 2%

profile of v1, /device:TPU:56, one launch (start us, length us, event | category | flops | bytes accessed | tf_op | source)
XLA Modules:
  0.0 378.1 jit_solution(15148111987078949183)
XLA Ops:
  0.6 0.0 copy-start.2
  0.6 1.5 broadcast_in_dim.100
  2.2 8.5 %all-to-all-start.6 = ((f32[16,8,256]{2,1,0:T(8,128)}), f32[16,8,256]{2,1,0:T(8,128)S(1)}, u32[]{:S(2)}, u32[]{:S(2)}) async-start(f32[16,8,256]{2,1,0:T(8,128)} %broadcast_in_dim.100), calls=%async_computation.6 | async-start | bytes 262144 | tf_op jit(solution)/shard_map/all_to_all | solution.py:21
  10.7 1.3 fusion
  12.6 3.7 all-to-all-done.6
  16.3 0.1 select_reduce_fusion.5
  16.4 0.1 broadcast_in_dim.103
  16.5 29.1 %all_to_all.63.gathered_ref.right_ref = f32[32,2,8,256]{3,2,1,0:T(8,128)S(1)} all-to-all(f32[32,2,8,256]{3,2,1,0:T(8,128)S(1)} %broadcast_in_dim.103), channel_id=1, replica_groups=mesh['node'=16,'cuts'=32] {'cuts'}, dimensions={0} | all-to-all | bytes 1048576 | tf_op jit(solution)/shard_map/all_to_all | solution.py:21
  45.6 0.0 copy-done.2
  45.6 2.0 mix_left.5
  47.6 56.5 %all_to_all.64.halfway_ref = f32[32,128,128]{2,1,0:T(8,128)S(1)} all-to-all(f32[32,128,128]{2,1,0:T(8,128)S(1)} %mix_left.5), channel_id=1, replica_groups=mesh['node'=16,'cuts'=32] {'cuts'}, dimensions={0} | all-to-all | bytes 4194304 | tf_op jit(solution)/shard_map/all_to_all | solution.py:152
  104.1 0.0 copy-start.3
  104.1 4.8 %mix_right.5 = (f32[8,256,256]{2,1,0:T(8,128)}, f32[256,256]{1,0:T(8,128)S(1)}) custom-call(f32[32,2,8,256]{3,2,1,0:T(8,128)S(1)} %all_to_all.63.gathered_ref.right_ref, f32[32,128,128]{2,1,0:T(8,128)S(1)} %all_to_all.64.halfway_ref), custom_call_target="tpu_custom_call" | custom-call | tf_op jit(solution)/shard_map/mix_right/pallas_call | solution.py:194
  108.9 16.5 %all_to_all.65 = f32[32,8,256]{2,1,0:T(8,128)S(1)} all-to-all(f32[32,8,256]{2,1,0:T(8,128)S(1)} %bitcast.17), channel_id=1, replica_groups=mesh['node'=16,'cuts'=32] {'cuts'}, dimensions={0} | all-to-all | bytes 524288 | tf_op jit(solution)/shard_map/all_to_all | solution.py:204
  125.5 0.7 broadcast_in_dim.105
  126.1 6.3 %all-to-all-start.10 = ((f32[16,8,256]{2,1,0:T(8,128)}), f32[16,8,256]{2,1,0:T(8,128)S(1)}, u32[]{:S(2)}, u32[]{:S(2)}) async-start(f32[16,8,256]{2,1,0:T(8,128)} %broadcast_in_dim.105), calls=%async_computation.10 | async-start | bytes 262144 | tf_op jit(solution)/shard_map/all_to_all | solution.py:21
  134.4 0.0 copy-done.3
  134.4 3.7 all-to-all-done.10
  138.1 0.1 select_reduce_fusion.3
  138.2 6.4 %conditional.2 = ((f32[8,256,256]{2,1,0:T(8,128)}, f32[8,256]{1,0:T(8,128)S(1)})) conditional(s32[]{:T(128)} %convert_element_type.19, (f32[8,256,256]{2,1,0:T(8,128)}, f32[8,256]{1,0:T(8,128)S(1)}) %tuple.21, (f32[2,8,256]{2,1,0:T(8,128)S(1)}, f32[8,256,256]{2,1,0:T(8,128)S(1)}) %tuple.39), branch_computations={%region_6.7_spmd, %region_7.9_spmd} | conditional | flops 8000063488 | bytes 17850456 | solution.py:295
  144.6 0.7 broadcast_in_dim.107
  145.3 112.7 %all-to-all-start.11 = ((f32[16,8,256]{2,1,0:T(8,128)}), f32[16,8,256]{2,1,0:T(8,128)S(1)}, u32[]{:S(2)}, u32[]{:S(2)}) async-start(f32[16,8,256]{2,1,0:T(8,128)} %broadcast_in_dim.107), calls=%async_computation.11 | async-start | bytes 262144 | tf_op jit(solution)/shard_map/all_to_all | solution.py:21
  257.9 5.7 %all-to-all-done.11 = f32[16,8,256]{2,1,0:T(8,128)S(1)} async-done(((f32[16,8,256]{2,1,0:T(8,128)}), f32[16,8,256]{2,1,0:T(8,128)S(1)}, u32[]{:S(2)}, u32[]{:S(2)}) %all-to-all-start.11) | async-done | bytes 131104 | tf_op jit(solution)/shard_map/all_to_all | solution.py:21
  263.6 0.1 select_reduce_fusion.1
  263.7 85.2 %conditional.3 = ((f32[8,256,256]{2,1,0:T(8,128)}, f32[8,256]{1,0:T(8,128)S(1)})) conditional(s32[]{:T(128)} %convert_element_type.18, (f32[8,256,256]{2,1,0:T(8,128)}, f32[8,256]{1,0:T(8,128)S(1)}) %get-tuple-element.58, (f32[2,8,256]{2,1,0:T(8,128)S(1)}, f32[8,256,256]{2,1,0:T(8,128)}) %tuple.38), branch_computations={%region_11.12_spmd, %region_12.14_spmd} | conditional | flops 8000063488 | bytes 17850456 | solution.py:295
  263.7 0.1 broadcast_in_dim.82
  263.8 16.8 %all_to_all.61.gathered_ref = f32[32,2,8,256]{3,2,1,0:T(8,128)S(1)} all-to-all(f32[32,2,8,256]{3,2,1,0:T(8,128)S(1)} %broadcast_in_dim.82), channel_id=1, replica_groups=mesh['node'=16,'cuts'=32] {'cuts'}, dimensions={0} | all-to-all | bytes 1048576 | tf_op jit(solution)/shard_map/cond/branch_1_fun/all_to_all | solution.py:21
  280.6 10.1 %mix_left.4 = f32[32,128,128]{2,1,0:T(8,128)S(1)} custom-call(f32[32,2,8,256]{3,2,1,0:T(8,128)S(1)} %all_to_all.61.gathered_ref, f32[8,256,256]{2,1,0:T(8,128)} %get-tuple-element.21.tensor_hbm), custom_call_target="tpu_custom_call" | custom-call | tf_op jit(solution)/shard_map/cond/branch_1_fun/mix_left/pallas_call | solution.py:138
  290.8 0.0 copy-start.1
  290.8 1.3 copy-done.1
  292.1 6.0 %all-to-all-start.4 = ((f32[32,128,128]{2,1,0:T(8,128)}), f32[32,128,128]{2,1,0:T(8,128)S(1)}, u32[]{:S(2)}, u32[]{:S(2)}) async-start(f32[32,128,128]{2,1,0:T(8,128)} %copy-done.1), calls=%async_computation.4 | async-start | bytes 4194304 | tf_op jit(solution)/shard_map/cond/branch_1_fun/all_to_all | solution.py:152
  298.1 6.9 %right_factor.3.right_ref = f32[256,256]{1,0:T(8,128)S(1)} custom-call(f32[32,2,8,256]{3,2,1,0:T(8,128)S(1)} %all_to_all.61.gathered_ref), custom_call_target="tpu_custom_call" | custom-call | flops 8000000000 | bytes 786432 | tf_op jit(solution)/shard_map/cond/branch_1_fun/right_factor/pallas_call | solution.py:162
  305.0 21.9 %all-to-all-done.4.halfway_ref = f32[32,128,128]{2,1,0:T(8,128)S(1)} async-done(((f32[32,128,128]{2,1,0:T(8,128)}), f32[32,128,128]{2,1,0:T(8,128)S(1)}, u32[]{:S(2)}, u32[]{:S(2)}) %all-to-all-start.4) | async-done | bytes 2097184 | tf_op jit(solution)/shard_map/cond/branch_1_fun/all_to_all | solution.py:152
  326.9 4.8 %mix_right.4 = (f32[8,256,256]{2,1,0:T(8,128)}, f32[256,256]{1,0:T(8,128)S(1)}) custom-call(f32[256,256]{1,0:T(8,128)S(1)} %right_factor.3.right_ref, f32[32,128,128]{2,1,0:T(8,128)S(1)} %all-to-all-done.4.halfway_ref), custom_call_target="tpu_custom_call" | custom-call | tf_op jit(solution)/shard_map/cond/branch_1_fun/mix_right/pallas_call | solution.py:194
  331.7 17.0 %all_to_all.62 = f32[32,8,256]{2,1,0:T(8,128)S(1)} all-to-all(f32[32,8,256]{2,1,0:T(8,128)S(1)} %bitcast.16), channel_id=1, replica_groups=mesh['node'=16,'cuts'=32] {'cuts'}, dimensions={0} | all-to-all | bytes 524288 | tf_op jit(solution)/shard_map/cond/branch_1_fun/all_to_all | solution.py:204
  349.0 0.7 broadcast_in_dim.108
  349.7 4.7 %all-to-all-start.12 = ((f32[32,8,256]{2,1,0:T(8,128)}), f32[32,8,256]{2,1,0:T(8,128)S(1)}, u32[]{:S(2)}, u32[]{:S(2)}) async-start(f32[32,8,256]{2,1,0:T(8,128)} %broadcast_in_dim.108), calls=%async_computation.12 | async-start | bytes 524288 | tf_op jit(solution)/shard_map/all_to_all | solution.py:21
  354.4 0.1 pad_add_fusion.place_ref
  354.4 10.7 %all-to-all-done.12.gathered_ref = f32[32,8,256]{2,1,0:T(8,128)S(1)} async-done(((f32[32,8,256]{2,1,0:T(8,128)}), f32[32,8,256]{2,1,0:T(8,128)S(1)}, u32[]{:S(2)}, u32[]{:S(2)}) %all-to-all-start.12) | async-done | bytes 262176 | tf_op jit(solution)/shard_map/all_to_all | solution.py:21
  365.2 12.4 %last.1 = (f32[256,8,256]{2,1,0:T(8,128)}, f32[8,256]{1,0:T(8,128)}) custom-call(s32[2]{0:T(128)S(1)} %pad_add_fusion.place_ref, f32[32,8,256]{2,1,0:T(8,128)S(1)} %all-to-all-done.12.gathered_ref, f32[8,256,256]{2,1,0:T(8,128)} %get-tuple-element.37.mixed_hbm), custom_call_target="tpu_custom_call" | custom-call | tf_op jit(solution)/shard_map/last/pallas_call | solution.py:237
  (7 shorter events, 0.1 us)
Async XLA Ops:
  0.6 45.0 %copy-start.2 = (f32[1,8,256,256]{3,2,1,0:T(8,128)S(1)}, f32[1,8,256,256]{3,2,1,0:T(8,128)}, u32[]{:S(2)}) copy-start(f32[1,8,256,256]{3,2,1,0:T(8,128)} %param.7) | copy-start | bytes 6291460
  2.2 14.2 %all-to-all-start.6 = ((f32[16,8,256]{2,1,0:T(8,128)}), f32[16,8,256]{2,1,0:T(8,128)S(1)}, u32[]{:S(2)}, u32[]{:S(2)}) async-start(f32[16,8,256]{2,1,0:T(8,128)} %broadcast_in_dim.100), calls=%async_computation.6 | async-start | bytes 262144 | tf_op jit(solution)/shard_map/all_to_all | solution.py:21
  104.1 30.3 %copy-start.3 = (s32[16]{0:T(128)S(1)}, s32[16]{0:T(128)}, u32[]{:S(2)}) copy-start(s32[16]{0:T(128)} %param.9) | copy-start | bytes 196
  126.1 12.0 %all-to-all-start.10 = ((f32[16,8,256]{2,1,0:T(8,128)}), f32[16,8,256]{2,1,0:T(8,128)S(1)}, u32[]{:S(2)}, u32[]{:S(2)}) async-start(f32[16,8,256]{2,1,0:T(8,128)} %broadcast_in_dim.105), calls=%async_computation.10 | async-start | bytes 262144 | tf_op jit(solution)/shard_map/all_to_all | solution.py:21
  145.3 118.3 %all-to-all-start.11 = ((f32[16,8,256]{2,1,0:T(8,128)}), f32[16,8,256]{2,1,0:T(8,128)S(1)}, u32[]{:S(2)}, u32[]{:S(2)}) async-start(f32[16,8,256]{2,1,0:T(8,128)} %broadcast_in_dim.107), calls=%async_computation.11 | async-start | bytes 262144 | tf_op jit(solution)/shard_map/all_to_all | solution.py:21
  290.8 1.3 copy-start.1
  292.1 34.8 %all-to-all-start.4 = ((f32[32,128,128]{2,1,0:T(8,128)}), f32[32,128,128]{2,1,0:T(8,128)S(1)}, u32[]{:S(2)}, u32[]{:S(2)}) async-start(f32[32,128,128]{2,1,0:T(8,128)} %copy-done.1), calls=%async_computation.4 | async-start | bytes 4194304 | tf_op jit(solution)/shard_map/cond/branch_1_fun/all_to_all | solution.py:152
  349.7 15.5 %all-to-all-start.12 = ((f32[32,8,256]{2,1,0:T(8,128)}), f32[32,8,256]{2,1,0:T(8,128)S(1)}, u32[]{:S(2)}, u32[]{:S(2)}) async-start(f32[32,8,256]{2,1,0:T(8,128)} %broadcast_in_dim.108), calls=%async_computation.12 | async-start | bytes 524288 | tf_op jit(solution)/shard_map/all_to_all | solution.py:21

commit v2 on v1

--- a/solution.py
+++ b/solution.py
@@ -96,16 +96,6 @@
                 work_ref[rows, end:] = jnp.zeros((PANEL, 2 * size - end), jnp.float32)
 
 
-def child_rows(gathered_ref, side):
-    size = gathered_ref.shape[-1]
-
-    def read_rows(first):
-        members = pl.ds(first // TILE, PANEL // TILE)
-        return gathered_ref[members, side].reshape(PANEL, size)
-
-    return read_rows
-
-
 def mix_tensor(left, tensor_ref, out_ref):
     count, size, _ = tensor_ref.shape
     for p in range(count):
@@ -117,57 +107,51 @@
                 ]
 
 
-def leaf_left_kernel(gathered_ref, tensor_ref, out_ref):
+def mix_left_kernel(left_ref, tensor_ref, out_ref):
     size = tensor_ref.shape[1]
-    mix_tensor(gathered_ref[:, 0].reshape(size, size), tensor_ref, out_ref)
-
-
-def inner_left_kernel(gathered_ref, tensor_hbm, out_ref, tensor_ref, work_ref, done):
-    size = tensor_ref.shape[1]
-    copy = pltpu.make_async_copy(tensor_hbm, tensor_ref, done)
-    copy.start()
-    factor_gram(child_rows(gathered_ref, 0), size, work_ref)
-    copy.wait()
-    mix_tensor(work_ref[...], tensor_ref, out_ref)
-
-
-def mix_left(gathered, tensor, inner):
+    if len(left_ref.shape) == 4:
+        left = left_ref[:, 0].reshape(size, size)
+    else:
+        left = left_ref[...]
+    mix_tensor(left, tensor_ref, out_ref)
+
+
+def mix_left(left, tensor):
     count, size, _ = tensor.shape
-    result = jax.ShapeDtypeStruct((size // TILE, size * count // 16, LANES), jnp.float32)
-    whole = pl.BlockSpec(memory_space=VMEM)
+    blocks, half = size // TILE, size // LANES
     mixed = pl.pallas_call(
-        inner_left_kernel if inner else leaf_left_kernel,
-        in_specs=[whole, pl.BlockSpec(memory_space=pl.ANY) if inner else whole],
-        out_shape=result,
-        scratch_shapes=[
-            VMEM(tensor.shape, jnp.float32),
-            VMEM((size, size), jnp.float32),
-            pltpu.SemaphoreType.DMA(()),
-        ]
-        if inner
-        else [],
+        mix_left_kernel,
+        out_shape=jax.ShapeDtypeStruct((blocks, half * TILE * count, LANES), jnp.float32),
         compiler_params=PARAMS,
         name="mix_left",
-    )(gathered, tensor)
+    )(left, tensor)
     return lax.all_to_all(mixed, "cuts", 0, 0, tiled=True)
 
 
-def right_factor_kernel(gathered_ref, out_ref):
+def child_factor_kernel(side_ref, gathered_ref, out_ref):
     size = out_ref.shape[0]
-    factor_gram(child_rows(gathered_ref, 1), size, out_ref)
-
-
-def right_factor(gathered):
+    side = side_ref[0]
+
+    def read_rows(first):
+        members = pl.ds(first // TILE, PANEL // TILE)
+        return gathered_ref[members, side].reshape(PANEL, size)
+
+    factor_gram(read_rows, size, out_ref)
+
+
+def child_factor(gathered, side):
     size = gathered.shape[-1]
+    whole = pl.BlockSpec(memory_space=VMEM)
     return pl.pallas_call(
-        right_factor_kernel,
+        child_factor_kernel,
+        in_specs=[pl.BlockSpec(memory_space=pltpu.SMEM), whole],
         out_shape=jax.ShapeDtypeStruct((size, size), jnp.float32),
         cost_estimate=pl.CostEstimate(
             flops=8 * 10**9, bytes_accessed=3 * 4 * size * size, transcendentals=size
         ),
         compiler_params=PARAMS,
-        name="right_factor",
-    )(gathered)
+        name="child_factor",
+    )(jnp.full((1,), side, jnp.int32), gathered)
 
 
 def mix_right_kernel(right_ref, halfway_ref, mixed_ref, gram_ref):
@@ -178,15 +162,23 @@
         right = right_ref[...]
     lines = mixed_ref.shape[0]
     parents = halfway_ref.shape[1] // (lines * (size // LANES))
-    for x in range(lines):
+
+    def add_line(x):
         halves = []
         for half in range(size // LANES):
-            rows = pl.ds((half * lines + x) * parents, parents)
-            halves.append(halfway_ref[:, rows, :].reshape(size, LANES))
+            start = pl.multiple_of((half * lines + x) * parents, parents)
+            halves.append(halfway_ref[:, pl.ds(start, parents), :].reshape(size, LANES))
         mixed = product(jnp.concatenate(halves, axis=1), right, (1, 1))
         mixed_ref[x] = mixed
-        term = product(mixed, mixed, (1, 1))
-        gram_ref[...] = term if x == 0 else gram_ref[...] + term
+        return product(mixed, mixed, (1, 1))
+
+    gram_ref[...] = jnp.zeros_like(gram_ref)
+
+    def add_lines(step, carry):
+        gram_ref[...] += add_line(2 * step) + add_line(2 * step + 1)
+        return carry
+
+    lax.fori_loop(0, lines // 2, add_lines, 0)
 
 
 def mix_right(halfway, right):
@@ -279,22 +271,22 @@
 
     rows = pick_children(leaf_factors[0], [slot_ids == child for child in children])
     gathered = from_everyone(rows, "cuts")
-    halfway = mix_left(gathered, tensor, inner=False)
+    halfway = mix_left(gathered, tensor)
     mixed, rows_here = mix_right(halfway, gathered)
 
     def process(rows, tensor, mixed, rows_here):
         gathered = from_everyone(rows, "cuts")
-        halfway = mix_left(gathered, tensor, inner=True)
-        return mix_right(halfway, right_factor(gathered))
+        halfway = mix_left(child_factor(gathered, 0), tensor)
+        return mix_right(halfway, child_factor(gathered, 1))
 
     def keep(rows, tensor, mixed, rows_here):
         return mixed, rows_here
 
-    for level_now in range(log_slots - 2, 0, -1):
-        rows = pick_children(rows_here, [node_of_slot == child for child in children])
-        mixed, rows_here = lax.cond(
-            my_depth == level_now, process, keep, rows, tensor, mixed, rows_here
-        )
+    def level(step, state):
+        rows = pick_children(state[1], [node_of_slot == child for child in children])
+        return lax.cond(my_depth == log_slots - 2 - step, process, keep, rows, tensor, *state)
+
+    mixed, rows_here = lax.fori_loop(0, log_slots - 2, level, (mixed, rows_here))
 
     gathered = from_everyone(rows_here, "cuts")
     basis, upper = last(place, gathered, mixed)

time: 371 us -> 395 us (1.065)
  the two profiles are of different devices: /device:TPU:56 before, /device:TPU:64 now
where the time goes in v2:
time: 395 us; the launch traced here: 394 us
  starting transfers between devices  142 us (36%)
  blocking collectives  123 us (31%)
  waiting for transfers between devices  67.7 us (17%)
  Pallas kernels  50 us (13%)
  local copies, waits for them, and re-layouts  4.83 us (1%)
    all_to_all x4, starting transfers between devices, from_everyone(): lax.all_to_all(jnp.broadcast_to(array[None], (count, *array.shape)), axis...  132 us
    all_to_all x1, blocking collectives, mix_left(): return lax.all_to_all(mixed, 'cuts', 0, 0, tiled=True)  55.3 us
    all_to_all x2, blocking collectives, from_everyone(): lax.all_to_all(jnp.broadcast_to(array[None], (count, *array.shape)), axis...  51.5 us
    all_to_all x4, waiting for transfers between devices, from_everyone(): lax.all_to_all(jnp.broadcast_to(array[None], (count, *array.shape)), axis...  34.8 us
    all_to_all x1, waiting for transfers between devices, mix_left(): return lax.all_to_all(mixed, 'cuts', 0, 0, tiled=True)  23.1 us
    pallas_call x2, Pallas kernels, mix_right(): pl.pallas_call(mix_right_kernel, out_shape=[jax.ShapeDtypeStruct((TILE, s...  16.7 us
    all_to_all x1, blocking collectives, mix_right(): lax.all_to_all(partial.reshape(cut_count, size // cut_count, size), 'cuts...  16 us
    pallas_call x2, Pallas kernels, child_factor(): pl.pallas_call(child_factor_kernel, in_specs=[pl.BlockSpec(memory_space=p...  13.8 us
  transfers between devices with their start and end apart: 6, of which 6 were waited for; matrix products, arithmetic and copies ran while one was open for 0% of the time, Pallas kernels for 2%

profile of v2, /device:TPU:64, one launch (start us, length us, event | category | flops | bytes accessed | tf_op | source)
XLA Modules:
  0.0 393.7 jit_solution(13650931948478463598)
XLA Ops:
  0.6 1.4 broadcast_in_dim.118
  2.0 7.2 %all-to-all-start.4 = ((f32[16,8,256]{2,1,0:T(8,128)}), f32[16,8,256]{2,1,0:T(8,128)S(1)}, u32[]{:S(2)}, u32[]{:S(2)}) async-start(f32[16,8,256]{2,1,0:T(8,128)} %broadcast_in_dim.118), calls=%async_computation.4 | async-start | bytes 262144 | tf_op jit(solution)/shard_map/all_to_all | solution.py:21
  9.2 1.3 fusion
  11.2 6.7 %all-to-all-done.4 = f32[16,8,256]{2,1,0:T(8,128)S(1)} async-done(((f32[16,8,256]{2,1,0:T(8,128)}), f32[16,8,256]{2,1,0:T(8,128)S(1)}, u32[]{:S(2)}, u32[]{:S(2)}) %all-to-all-start.4) | async-done | bytes 131104 | tf_op jit(solution)/shard_map/all_to_all | solution.py:21
  17.9 0.1 select_reduce_fusion.3
  18.0 0.1 broadcast_in_dim.121
  18.0 30.9 %all_to_all.49.left_ref.right_ref = f32[32,2,8,256]{3,2,1,0:T(8,128)S(1)} all-to-all(f32[32,2,8,256]{3,2,1,0:T(8,128)S(1)} %broadcast_in_dim.121), channel_id=1, replica_groups=mesh['node'=16,'cuts'=32] {'cuts'}, dimensions={0} | all-to-all | bytes 1048576 | tf_op jit(solution)/shard_map/all_to_all | solution.py:21
  48.9 3.6 mix_left.3
  52.5 55.3 %all_to_all.50.halfway_ref = f32[32,128,128]{2,1,0:T(8,128)S(1)} all-to-all(f32[32,128,128]{2,1,0:T(8,128)S(1)} %mix_left.3), channel_id=1, replica_groups=mesh['node'=16,'cuts'=32] {'cuts'}, dimensions={0} | all-to-all | bytes 4194304 | tf_op jit(solution)/shard_map/all_to_all | solution.py:128
  107.8 0.0 copy-start.1
  107.8 8.5 %mix_right.3 = (f32[8,256,256]{2,1,0:T(8,128)}, f32[256,256]{1,0:T(8,128)}) custom-call(f32[32,2,8,256]{3,2,1,0:T(8,128)S(1)} %all_to_all.49.left_ref.right_ref, f32[32,128,128]{2,1,0:T(8,128)S(1)} %all_to_all.50.halfway_ref), custom_call_target="tpu_custom_call" | custom-call | tf_op jit(solution)/shard_map/mix_right/pallas_call | solution.py:186
  116.3 5.2 %all-to-all-start.7 = ((f32[32,8,256]{2,1,0:T(8,128)}), f32[32,8,256]{2,1,0:T(8,128)S(1)}, u32[]{:S(2)}, u32[]{:S(2)}) async-start(f32[32,8,256]{2,1,0:T(8,128)} %bitcast.9), calls=%async_computation.7 | async-start | bytes 524288 | tf_op jit(solution)/shard_map/all_to_all | solution.py:196
  123.4 9.8 %all-to-all-done.7 = f32[32,8,256]{2,1,0:T(8,128)S(1)} async-done(((f32[32,8,256]{2,1,0:T(8,128)}), f32[32,8,256]{2,1,0:T(8,128)S(1)}, u32[]{:S(2)}, u32[]{:S(2)}) %all-to-all-start.7) | async-done | bytes 262176 | tf_op jit(solution)/shard_map/all_to_all | solution.py:196
  133.3 0.0 copy-done.1
  133.3 231.5 %while.15 = (s32[]{:T(128)}, f32[8,256,256]{2,1,0:T(8,128)}, f32[8,256]{1,0:T(8,128)S(1)}, s32[]{:T(128)}, s32[]{:T(128)}, /*index=5*/s32[16]{0:T(128)S(1)}, s32...) while((s32[]{:T(128)}, f32[8,256,256]{2,1,0:T(8,128)}, f32[8,256]{1,0:T(8,128)S(1)}, s32[]{:T(128)}, ...), condition=%wide.region_10.11_spmd, body=%wide.region_4.10_spmd.sunk | while | flops 16000194560 | bytes 19349920 | solution.py:289
  133.5 0.7 broadcast_in_dim.139
  134.2 3.5 all-to-all-start.3
  137.7 8.6 %all-to-all-done.3 = f32[16,8,256]{2,1,0:T(8,128)S(1)} async-done(((f32[16,8,256]{2,1,0:T(8,128)}), f32[16,8,256]{2,1,0:T(8,128)S(1)}, u32[]{:S(2)}, u32[]{:S(2)}) %all-to-all-start.3) | async-done | bytes 131104 | tf_op jit(solution)/shard_map/while/body/eval_jaxpr/all_to_all | solution.py:21
  146.3 0.1 select_reduce_fusion.5
  146.5 0.7 broadcast_in_dim.139
  147.1 117.2 %all-to-all-start.3 = ((f32[16,8,256]{2,1,0:T(8,128)}), f32[16,8,256]{2,1,0:T(8,128)S(1)}, u32[]{:S(2)}, u32[]{:S(2)}) async-start(f32[16,8,256]{2,1,0:T(8,128)} %broadcast_in_dim.139), calls=%async_computation.3 | async-start | bytes 262144 | tf_op jit(solution)/shard_map/while/body/eval_jaxpr/all_to_all | solution.py:21
  264.4 8.6 %all-to-all-done.3 = f32[16,8,256]{2,1,0:T(8,128)S(1)} async-done(((f32[16,8,256]{2,1,0:T(8,128)}), f32[16,8,256]{2,1,0:T(8,128)S(1)}, u32[]{:S(2)}, u32[]{:S(2)}) %all-to-all-start.3) | async-done | bytes 131104 | tf_op jit(solution)/shard_map/while/body/eval_jaxpr/all_to_all | solution.py:21
  273.0 0.1 select_reduce_fusion.5
  273.1 91.5 %conditional.2 = ((f32[8,256,256]{2,1,0:T(8,128)}, f32[8,256]{1,0:T(8,128)S(1)})) conditional(s32[]{:T(128)} %convert_element_type.20, (f32[8,256,256]{2,1,0:T(8,128)}, f32[8,256]{1,0:T(8,128)S(1)}) %tuple.49, (f32[2,8,256]{2,1,0:T(8,128)S(1)}, f32[8,256,256]{2,1,0:T(8,128)}) %tuple.50), branch_computations={%region_7.7_spmd, %region_8.9_spmd} | conditional | flops 16000063488 | bytes 18636888 | solution.py:287
  273.1 0.1 broadcast_in_dim.100
  273.2 20.6 %all_to_all.47.gathered_ref = f32[32,2,8,256]{3,2,1,0:T(8,128)S(1)} all-to-all(f32[32,2,8,256]{3,2,1,0:T(8,128)S(1)} %broadcast_in_dim.100), channel_id=1, replica_groups=mesh['node'=16,'cuts'=32] {'cuts'}, dimensions={0} | all-to-all | bytes 1048576 | tf_op jit(solution)/shard_map/while/body/eval_jaxpr/cond/branch_1_fun/all_to_all | solution.py:21
  293.8 6.9 %child_factor.3.left_ref = f32[256,256]{1,0:T(8,128)S(1)} custom-call(s32[1]{0:T(128)} %constant.48.clone.side_ref, f32[32,2,8,256]{3,2,1,0:T(8,128)S(1)} %all_to_all.47.gathered_ref), custom_call_target="tpu_custom_call" | custom-call | flops 8000000000 | bytes 786432 | tf_op jit(solution)/shard_map/while/body/eval_jaxpr/cond/branch_1_fun/child_factor/pallas_call | solution.py:145
  300.7 3.6 mix_left.2
  304.3 0.0 copy-start
  304.3 1.3 copy-done
  305.6 4.8 %all-to-all-start.1 = ((f32[32,128,128]{2,1,0:T(8,128)}), f32[32,128,128]{2,1,0:T(8,128)S(1)}, u32[]{:S(2)}, u32[]{:S(2)}) async-start(f32[32,128,128]{2,1,0:T(8,128)} %copy-done), calls=%async_computation.1 | async-start | bytes 4194304 | tf_op jit(solution)/shard_map/while/body/eval_jaxpr/cond/branch_1_fun/all_to_all | solution.py:128
  310.4 6.9 %child_factor.2.right_ref = f32[256,256]{1,0:T(8,128)S(1)} custom-call(s32[1]{0:T(128)} %constant.47.clone.side_ref, f32[32,2,8,256]{3,2,1,0:T(8,128)S(1)} %all_to_all.47.gathered_ref), custom_call_target="tpu_custom_call" | custom-call | flops 8000000000 | bytes 786432 | tf_op jit(solution)/shard_map/while/body/eval_jaxpr/cond/branch_1_fun/child_factor/pallas_call | solution.py:145
  317.3 23.1 %all-to-all-done.1.halfway_ref = f32[32,128,128]{2,1,0:T(8,128)S(1)} async-done(((f32[32,128,128]{2,1,0:T(8,128)}), f32[32,128,128]{2,1,0:T(8,128)S(1)}, u32[]{:S(2)}, u32[]{:S(2)}) %all-to-all-start.1) | async-done | bytes 2097184 | tf_op jit(solution)/shard_map/while/body/eval_jaxpr/cond/branch_1_fun/all_to_all | solution.py:128
  340.4 8.2 %mix_right.2 = (f32[8,256,256]{2,1,0:T(8,128)}, f32[256,256]{1,0:T(8,128)S(1)}) custom-call(f32[256,256]{1,0:T(8,128)S(1)} %child_factor.2.right_ref, f32[32,128,128]{2,1,0:T(8,128)S(1)} %all-to-all-done.1.halfway_ref), custom_call_target="tpu_custom_call" | custom-call | tf_op jit(solution)/shard_map/while/body/eval_jaxpr/cond/branch_1_fun/mix_right/pallas_call | solution.py:186
  348.6 16.0 %all_to_all.48 = f32[32,8,256]{2,1,0:T(8,128)S(1)} all-to-all(f32[32,8,256]{2,1,0:T(8,128)S(1)} %bitcast.16), channel_id=1, replica_groups=mesh['node'=16,'cuts'=32] {'cuts'}, dimensions={0} | all-to-all | bytes 524288 | tf_op jit(solution)/shard_map/while/body/eval_jaxpr/cond/branch_1_fun/all_to_all | solution.py:196
  364.9 0.7 broadcast_in_dim.122
  365.6 4.5 %all-to-all-start.8 = ((f32[32,8,256]{2,1,0:T(8,128)}), f32[32,8,256]{2,1,0:T(8,128)S(1)}, u32[]{:S(2)}, u32[]{:S(2)}) async-start(f32[32,8,256]{2,1,0:T(8,128)} %broadcast_in_dim.122), calls=%async_computation.8 | async-start | bytes 524288 | tf_op jit(solution)/shard_map/all_to_all | solution.py:21
  370.1 0.1 pad_add_fusion.place_ref
  370.2 10.9 %all-to-all-done.8.gathered_ref = f32[32,8,256]{2,1,0:T(8,128)S(1)} async-done(((f32[32,8,256]{2,1,0:T(8,128)}), f32[32,8,256]{2,1,0:T(8,128)S(1)}, u32[]{:S(2)}, u32[]{:S(2)}) %all-to-all-start.8) | async-done | bytes 262176 | tf_op jit(solution)/shard_map/all_to_all | solution.py:21
  381.1 12.4 %last.1 = (f32[256,8,256]{2,1,0:T(8,128)}, f32[8,256]{1,0:T(8,128)}) custom-call(s32[2]{0:T(128)S(1)} %pad_add_fusion.place_ref, f32[32,8,256]{2,1,0:T(8,128)S(1)} %all-to-all-done.8.gathered_ref, f32[8,256,256]{2,1,0:T(8,128)} %get-tuple-element.167.mixed_hbm), custom_call_target="tpu_custom_call" | custom-call | tf_op jit(solution)/shard_map/last/pallas_call | solution.py:229
  (9 shorter events, 0.1 us)
Async XLA Ops:
  2.0 15.9 %all-to-all-start.4 = ((f32[16,8,256]{2,1,0:T(8,128)}), f32[16,8,256]{2,1,0:T(8,128)S(1)}, u32[]{:S(2)}, u32[]{:S(2)}) async-start(f32[16,8,256]{2,1,0:T(8,128)} %broadcast_in_dim.118), calls=%async_computation.4 | async-start | bytes 262144 | tf_op jit(solution)/shard_map/all_to_all | solution.py:21
  107.8 25.5 %copy-start.1 = (s32[16]{0:T(128)S(1)}, s32[16]{0:T(128)}, u32[]{:S(2)}) copy-start(s32[16]{0:T(128)} %param.9) | copy-start | bytes 196
  116.3 17.0 %all-to-all-start.7 = ((f32[32,8,256]{2,1,0:T(8,128)}), f32[32,8,256]{2,1,0:T(8,128)S(1)}, u32[]{:S(2)}, u32[]{:S(2)}) async-start(f32[32,8,256]{2,1,0:T(8,128)} %bitcast.9), calls=%async_computation.7 | async-start | bytes 524288 | tf_op jit(solution)/shard_map/all_to_all | solution.py:196
  134.2 12.1 %all-to-all-start.3 = ((f32[16,8,256]{2,1,0:T(8,128)}), f32[16,8,256]{2,1,0:T(8,128)S(1)}, u32[]{:S(2)}, u32[]{:S(2)}) async-start(f32[16,8,256]{2,1,0:T(8,128)} %broadcast_in_dim.139), calls=%async_computation.3 | async-start | bytes 262144 | tf_op jit(solution)/shard_map/while/body/eval_jaxpr/all_to_all | solution.py:21
  147.1 125.9 %all-to-all-start.3 = ((f32[16,8,256]{2,1,0:T(8,128)}), f32[16,8,256]{2,1,0:T(8,128)S(1)}, u32[]{:S(2)}, u32[]{:S(2)}) async-start(f32[16,8,256]{2,1,0:T(8,128)} %broadcast_in_dim.139), calls=%async_computation.3 | async-start | bytes 262144 | tf_op jit(solution)/shard_map/while/body/eval_jaxpr/all_to_all | solution.py:21
  304.3 1.3 copy-start
  305.6 34.8 %all-to-all-start.1 = ((f32[32,128,128]{2,1,0:T(8,128)}), f32[32,128,128]{2,1,0:T(8,128)S(1)}, u32[]{:S(2)}, u32[]{:S(2)}) async-start(f32[32,128,128]{2,1,0:T(8,128)} %copy-done), calls=%async_computation.1 | async-start | bytes 4194304 | tf_op jit(solution)/shard_map/while/body/eval_jaxpr/cond/branch_1_fun/all_to_all | solution.py:128
  365.6 15.5 %all-to-all-start.8 = ((f32[32,8,256]{2,1,0:T(8,128)}), f32[32,8,256]{2,1,0:T(8,128)S(1)}, u32[]{:S(2)}, u32[]{:S(2)}) async-start(f32[32,8,256]{2,1,0:T(8,128)} %broadcast_in_dim.122), calls=%async_computation.8 | async-start | bytes 524288 | tf_op jit(solution)/shard_map/all_to_all | solution.py:21
